TPU v7x, 32 devices: a whole 2x2x4 slice. The times are simulated.
32 devices in a mesh: gx: 8 (over z, core), gy: 4 (over y, x).
Axes of the slice: x: 2, y: 2, z: 4, core: 2. Of those that a mesh axis runs over, the one named last changes fastest.
Arguments:
- grid_field: bfloat16 [1, 20, 2048, 2048], P(None, None, 'gx', 'gy'), may hold values from -8 to 8
- spectral_weight: float32 [2, 2, 20, 20, 2048], P(None, None, None, None, ('gx', 'gy')), may hold values from -1 to 1
- conv_near: bfloat16 [2, 20, 180], replicated, may hold values from -0.4375 to 0.4375
- conv_far: bfloat16 [2, 20, 500], replicated, may hold values from -0.25 to 0.25
- mix_logits: float32 [2, 3], replicated, may hold values from -1 to 1
- channel_bias: float32 [2, 20], replicated, may hold values from -3 to 3
Outputs:
- result_field: bfloat16 [1, 20, 2048, 2048], P(None, None, 'gx', 'gy')
All inputs are finite; a program needn't handle non-finite values.
Results may differ from a plain program's by a relative error of at most 0.004.
Values may be sent and summed in bfloat16 or wider, within the bound.
A program may use at most 448 MiB of HBM per device.

v0:
```python
import math

import jax
import jax.numpy as jnp
from jax import lax
from jax.sharding import PartitionSpec as P

NX = 2048
NY = 2048
MX = 32
MY = 32
LAYERS = 2
KX = 64
MODES = 2048


full_turn = 2.0 * math.pi
highest = lax.Precision.HIGHEST


def padded_2(value, sides, width):
    for axis, dim in sides:
        size, length = (lax.axis_size(axis), value.shape[dim])
        up = [(i, (i + 1) % size) for i in range(size)]
        down = [(j, i) for i, j in up]
        last = lax.slice_in_dim(value, length - width, length, axis=dim)
        first = lax.slice_in_dim(value, 0, width, axis=dim)
        before = lax.ppermute(last, axis, up)
        after = lax.ppermute(first, axis, down)
        value = jnp.concatenate([before, value, after], axis=dim)
    return value


def forward_table(positions):
    col_modes = jnp.arange(MY, dtype=jnp.int32)
    phases = (positions[:, None] * col_modes[None, :] % NY).astype(jnp.float32) * (full_turn / NY)
    return jnp.concatenate([jnp.cos(phases), -jnp.sin(phases)], axis=1).astype(jnp.bfloat16)


def row_tables(positions):
    lower = jnp.arange(MX, dtype=jnp.int32)
    row_modes = jnp.concatenate([lower, lower + (NX - MX)])
    phases = (positions[:, None] * row_modes[None, :] % NX).astype(jnp.float32) * (full_turn / NX)
    return (jnp.cos(phases), jnp.sin(phases))


def inverse_table(positions):
    col_modes = jnp.arange(MY, dtype=jnp.int32)
    col_weight = jnp.where(col_modes == 0, 1.0, 2.0).astype(jnp.float32) / (NX * NY)
    phases = (col_modes[:, None] * positions[None, :] % NY).astype(jnp.float32) * (full_turn / NY)
    return jnp.concatenate(
        [jnp.cos(phases) * col_weight[:, None], -jnp.sin(phases) * col_weight[:, None]], axis=0
    )


def conv_rows(padded_plane, tap_weights, dilation, side_taps, first_row, count_rows, local_cols):
    channels = padded_plane.shape[0]
    pieces = []
    for row_tap in range(side_taps):
        for col_tap in range(side_taps):
            row_offset = 4 + (row_tap - side_taps // 2) * dilation + first_row
            col_offset = 4 + (col_tap - side_taps // 2) * dilation
            pieces.append(
                padded_plane[
                    :, row_offset : row_offset + count_rows, col_offset : col_offset + local_cols
                ]
            )
    stacked = jnp.stack(pieces, 0)
    shaped_weights = tap_weights.reshape(channels, side_taps * side_taps, channels)
    return jnp.einsum("otc,tcxy->oxy", shaped_weights, stacked, preferred_element_type=jnp.float32)


def on_device(grid_field, spectral_weight, conv_near, conv_far, mix_logits, channel_bias):
    channels = grid_field.shape[1]
    local_rows = grid_field.shape[2]
    local_cols = grid_field.shape[3]
    row_positions = lax.axis_index("gx") * local_rows + jnp.arange(local_rows, dtype=jnp.int32)
    col_positions = lax.axis_index("gy") * local_cols + jnp.arange(local_cols, dtype=jnp.int32)
    forward_cols = forward_table(col_positions)
    cosine_rows, sine_rows = row_tables(row_positions)
    inverse_cols = inverse_table(col_positions)
    share_modes = spectral_weight.shape[-1]
    device_count = lax.axis_size("gx") * lax.axis_size("gy")
    row_blocks = max(1, local_rows // 32)
    while local_rows % row_blocks != 0:
        row_blocks = row_blocks - 1
    block_rows = local_rows // row_blocks
    planes_block = grid_field
    for layer_index in range(LAYERS):
        planes_here = planes_block.shape[0]
        line_sums = jnp.dot(
            planes_block.reshape(planes_here * channels * local_rows, local_cols),
            forward_cols,
            preferred_element_type=jnp.float32,
        )
        line_sums = line_sums.reshape(planes_here, channels, local_rows, 2 * MY)
        real_lines = line_sums[..., :MY]
        imaginary_lines = line_sums[..., MY:]

        def contract_rows(operand, lookup):
            return jnp.einsum("pcxk,xj->pcjk", operand, lookup, precision=highest)

        real_spec = contract_rows(real_lines, cosine_rows) + contract_rows(
            imaginary_lines, sine_rows
        )
        imaginary_spec = contract_rows(imaginary_lines, cosine_rows) - contract_rows(
            real_lines, sine_rows
        )
        partial_value = jnp.stack(
            [
                real_spec.reshape(planes_here, channels, MODES),
                imaginary_spec.reshape(planes_here, channels, MODES),
            ]
        )
        by_owner = jnp.transpose(
            partial_value.reshape(2, planes_here, channels, device_count, share_modes),
            (3, 0, 1, 2, 4),
        )
        own_modes = lax.psum_scatter(by_owner, ("gx", "gy"), scatter_dimension=0, tiled=True)[0]

        def mix_modes(spectrum, weights):
            return jnp.einsum("pcm,com->pom", spectrum, weights, precision=highest)

        weight_real = spectral_weight[layer_index, 0]
        weight_imaginary = spectral_weight[layer_index, 1]
        real_mixed = mix_modes(own_modes[0], weight_real) - mix_modes(
            own_modes[1], weight_imaginary
        )
        imaginary_mixed = mix_modes(own_modes[1], weight_real) + mix_modes(
            own_modes[0], weight_imaginary
        )
        own_block = jnp.stack([real_mixed, imaginary_mixed])[None]
        gathered = lax.all_gather(own_block, ("gx", "gy"), axis=0, tiled=True)
        gathered = jnp.transpose(gathered, (1, 2, 3, 0, 4)).reshape(2, planes_here, channels, MODES)
        real_full = gathered[0].reshape(planes_here, channels, KX, MY)
        imaginary_full = gathered[1].reshape(planes_here, channels, KX, MY)

        def expand_rows(spectrum, lookup):
            return jnp.einsum("pcjk,xj->pcxk", spectrum, lookup, precision=highest)

        real_rows = expand_rows(real_full, cosine_rows) - expand_rows(imaginary_full, sine_rows)
        imaginary_rows = expand_rows(real_full, sine_rows) + expand_rows(
            imaginary_full, cosine_rows
        )
        stacked = jnp.concatenate([real_rows, imaginary_rows], axis=-1).reshape(
            planes_here * channels * local_rows, 2 * MY
        )
        spectral = jnp.dot(stacked, inverse_cols, precision=highest)
        layer_spectral = spectral.reshape(planes_here, channels, local_rows, local_cols)
        padded = padded_2(planes_block, (("gx", 2), ("gy", 3)), 4)
        exponents = jnp.exp(mix_logits[layer_index])
        mixture = exponents / jnp.sum(exponents)
        bias_column = channel_bias[layer_index][:, None, None]
        row_pieces = []
        for block_index in range(row_blocks):
            first_row = block_index * block_rows
            near_term = conv_rows(
                padded[0], conv_near[layer_index], 1, 3, first_row, block_rows, local_cols
            )
            far_term = conv_rows(
                padded[0], conv_far[layer_index], 2, 5, first_row, block_rows, local_cols
            )
            spectral_rows = layer_spectral[0, :, first_row : first_row + block_rows, :]
            summed = (
                mixture[0] * spectral_rows
                + mixture[1] * near_term
                + mixture[2] * far_term
                + bias_column
            )
            row_pieces.append(jax.nn.gelu(summed, approximate=False).astype(jnp.bfloat16))
        outputs = [jnp.concatenate(row_pieces, axis=1)]
        planes_block = jnp.stack(outputs)
    return planes_block


def solution(mesh):
    in_specs = (
        P(None, None, "gx", "gy"),
        P(None, None, None, None, ("gx", "gy")),
        P(),
        P(),
        P(),
        P(),
    )
    out_specs = P(None, None, "gx", "gy")
    return jax.shard_map(
        on_device, mesh=mesh, in_specs=in_specs, out_specs=out_specs, check_vma=False
    )
```

profile of v0, /device:TPU:0, one launch (start us, length us, event | category | flops | bytes accessed | tf_op | source)
XLA Modules:
  0.0 1093.7 jit_solution(308368122212594458)
XLA Ops:
  30.7 6.0 constant_dynamic-update-slice_fusion.1
  58.9 7.4 maximum_bitcast_fusion
  86.0 7.3 constant_dynamic-update-slice_fusion.239
  93.3 5.8 constant_dynamic-update-slice_fusion.238
  160.7 5.1 constant_dynamic-update-slice_fusion.248
  215.2 5.9 convolution_bitcast_fusion.15
  226.9 5.1 constant_dynamic-update-slice_fusion.244
  237.0 5.0 constant_dynamic-update-slice_fusion.242
  242.1 5.3 constant_dynamic-update-slice_fusion.241
  249.7 9.4 convolution_bitcast_fusion.10
  259.1 9.4 convolution_bitcast_fusion.4
  269.6 9.5 convolution_bitcast_fusion.5
  280.3 9.4 convolution_bitcast_fusion.6
  289.6 9.4 convolution_bitcast_fusion.7
  310.1 9.7 convolution_bitcast_fusion.3
  341.7 9.6 convolution_bitcast_fusion.8
  351.3 9.5 convolution_bitcast_fusion.9
  365.1 67.6 %all-gather = f32[64,1,20,64]{3,1,2,0:T(1,128)S(1)} all-gather(f32[2,1,20,64]{3,1,2,0:T(1,128)S(1)} %pad_maximum_fusion.6), channel_id=2, replica_groups=mesh['gx'=8,'gy'=4] {'gx','gy'}, dimensions={0}, use_global_device_ids=true | all-gather | bytes 337920 | tf_op jit(solution)/shard_map/all_gather | solution.py:133
  449.1 8.8 convolution_bitcast_fusion.2
  457.9 6.1 constant_dynamic-update-slice_fusion.282
  464.0 6.2 constant_dynamic-update-slice_fusion.281
  470.2 6.1 constant_dynamic-update-slice_fusion.280
  476.4 5.9 constant_dynamic-update-slice_fusion.279
  482.4 5.9 constant_dynamic-update-slice_fusion.278
  488.4 6.3 constant_dynamic-update-slice_fusion.277
  494.7 5.8 constant_dynamic-update-slice_fusion.276
  500.6 5.8 constant_dynamic-update-slice_fusion.275
  530.5 8.4 maximum_bitcast_fusion.1
  571.1 5.1 constant_dynamic-update-slice_fusion.514
  618.7 5.3 constant_dynamic-update-slice_fusion.529
  624.0 7.4 constant_dynamic-update-slice_fusion.528
  631.4 7.0 constant_dynamic-update-slice_fusion.527
  638.3 6.3 constant_dynamic-update-slice_fusion.526
  644.6 5.5 constant_dynamic-update-slice_fusion.525
  652.5 6.4 constant_dynamic-update-slice_fusion.392
  658.9 5.2 constant_dynamic-update-slice_fusion.391
  664.1 5.4 constant_dynamic-update-slice_fusion.390
  669.5 6.4 constant_dynamic-update-slice_fusion.389
  675.9 6.5 constant_dynamic-update-slice_fusion.388
  682.4 6.2 constant_dynamic-update-slice_fusion.387
  693.6 5.6 constant_dynamic-update-slice_fusion.385
  717.2 5.9 constant_dynamic-update-slice_fusion.524
  723.1 6.1 constant_dynamic-update-slice_fusion.523
  729.2 6.6 constant_dynamic-update-slice_fusion.522
  735.7 6.0 constant_dynamic-update-slice_fusion.521
  750.7 17.2 %fusion.74 = f32[32,512,20]{1,2,0:T(8,128)} fusion(bf16[25,20,32,512]{3,2,1,0:T(8,128)(2,1)} %get-tuple-element.280, bf16[20,25,20]{1,0,2:T(8,128)(2,1)S(1)} %copy-done.55), kind=kOutput, calls=%fused_computation.67 | convolution fusion | flops 327680000 | bytes 17714720 | tf_op jit(solution)/shard_map/otc,tcxy->oxy/dot_general | solution.py:70
  768.0 17.4 %fusion.71 = f32[32,512,20]{1,2,0:T(8,128)} fusion(bf16[25,20,32,512]{3,2,1,0:T(8,128)(2,1)} %get-tuple-element.282, bf16[20,25,20]{1,0,2:T(8,128)(2,1)S(1)} %copy-done.55), kind=kOutput, calls=%fused_computation.66 | convolution fusion | flops 327680000 | bytes 17714720 | tf_op jit(solution)/shard_map/otc,tcxy->oxy/dot_general | solution.py:70
  789.8 17.0 %fusion.68 = f32[32,512,20]{1,2,0:T(8,128)} fusion(bf16[25,20,32,512]{3,2,1,0:T(8,128)(2,1)} %get-tuple-element.284, bf16[20,25,20]{1,0,2:T(8,128)(2,1)S(1)} %copy-done.55), kind=kOutput, calls=%fused_computation.65 | convolution fusion | flops 327680000 | bytes 17714720 | tf_op jit(solution)/shard_map/otc,tcxy->oxy/dot_general | solution.py:70
  806.8 17.7 %fusion.65 = f32[32,512,20]{1,2,0:T(8,128)} fusion(bf16[25,20,32,512]{3,2,1,0:T(8,128)(2,1)} %get-tuple-element.286, bf16[20,25,20]{1,0,2:T(8,128)(2,1)S(1)} %copy-done.55), kind=kOutput, calls=%fused_computation.64 | convolution fusion | flops 327680000 | bytes 17714720 | tf_op jit(solution)/shard_map/otc,tcxy->oxy/dot_general | solution.py:70
  837.2 17.2 %fusion.77 = f32[32,512,20]{1,2,0:T(8,128)} fusion(bf16[25,20,32,512]{3,2,1,0:T(8,128)(2,1)} %get-tuple-element.354, bf16[20,25,20]{1,0,2:T(8,128)(2,1)S(1)} %copy-done.55), kind=kOutput, calls=%fused_computation.68 | convolution fusion | flops 327680000 | bytes 17714720 | tf_op jit(solution)/shard_map/otc,tcxy->oxy/dot_general | solution.py:70
  882.5 5.2 constant_dynamic-update-slice_fusion.365
  905.6 10.0 fusion.62
  915.6 17.3 %fusion.59 = f32[32,512,20]{1,2,0:T(8,128)} fusion(bf16[25,20,32,512]{3,2,1,0:T(8,128)(2,1)} %get-tuple-element.500, bf16[20,25,20]{1,0,2:T(8,128)(2,1)S(1)} %copy-done.55), kind=kOutput, calls=%fused_computation.62 | convolution fusion | flops 327680000 | bytes 17714720 | tf_op jit(solution)/shard_map/otc,tcxy->oxy/dot_general | solution.py:70
  932.9 9.8 fusion.56
  948.6 70.9 %all-gather.1 = f32[64,1,20,64]{3,1,2,0:T(1,128)S(1)} all-gather(f32[2,1,20,64]{3,1,2,0:T(1,128)S(1)} %pad_maximum_fusion.7), channel_id=3, replica_groups=mesh['gx'=8,'gy'=4] {'gx','gy'}, dimensions={0}, use_global_device_ids=true | all-gather | bytes 337920 | tf_op jit(solution)/shard_map/all_gather | solution.py:133
  1026.5 8.5 convolution_bitcast_fusion.1
  1035.1 6.1 constant_dynamic-update-slice_fusion.562
  1041.2 6.2 constant_dynamic-update-slice_fusion.561
  1047.4 6.1 constant_dynamic-update-slice_fusion.560
  1053.6 6.1 constant_dynamic-update-slice_fusion.559
  1059.8 6.2 constant_dynamic-update-slice_fusion.558
  1066.0 6.4 constant_dynamic-update-slice_fusion.557
  1072.4 5.9 constant_dynamic-update-slice_fusion.556
  1078.3 5.9 constant_dynamic-update-slice_fusion.555
  (454 shorter events, 456.5 us)
Async XLA Ops:
  6.5 356.6 %all-reduce.5.cloned.1.call-start = ((), (), s32[]{:S(2)}) async-start(), calls=%async_computation | async-start | bytes 1310720
  7.6 23.1 %collective-permute-start = (bf16[1,20,4,512]{3,1,2,0:T(8,128)(2,1)S(1)}, bf16[1,20,4,512]{3,1,2,0:T(8,128)(2,1)S(1)}, u32[]{:S(2)}, u32[]{:S(2)}) collective-permute-start(bf16[1,20,4,512]{3,1,2,0:T(8,128)(2,1)S(1)} %copy.914), channel_id=1, source_target_pairs={{0,4},{4,8},{8,12},{12,16},{16,20},{20,24},{24,28},{28,0},{1,5},{5... | collective-permute-start | bytes 245768 | tf_op jit(solution)/shard_map/ppermute | solution.py:28
  8.2 28.5 %collective-permute-start.1 = (bf16[1,20,4,512]{3,1,2,0:T(8,128)(2,1)S(1)}, bf16[1,20,4,512]{3,1,2,0:T(8,128)(2,1)S(1)}, u32[]{:S(2)}, u32[]{:S(2)}) collective-permute-start(bf16[1,20,4,512]{3,1,2,0:T(8,128)(2,1)S(1)} %copy.915), channel_id=1, source_target_pairs={{4,0},{8,4},{12,8},{16,12},{20,16},{24,20},{28,24},{0,28},{5,1},{9... | collective-permute-start | bytes 245768 | tf_op jit(solution)/shard_map/ppermute | solution.py:29
  21.3 9.3 copy-start.57
  24.7 922.8 %all-reduce.7.cloned.1.call-start = ((), (), s32[]{:S(2)}) async-start(), calls=%async_computation.1 | async-start | bytes 1310720
  45.1 10.7 collective-permute-start.3
  48.1 5.3 collective-permute-start.2
  66.3 18.1 %copy-start = (bf16[20,264,520]{2,0,1:T(8,128)(2,1)}, bf16[20,264,520]{2,0,1:T(8,128)(2,1)S(1)}, u32[]{:S(2)}) copy-start(bf16[20,264,520]{2,0,1:T(8,128)(2,1)S(1)} %maximum_bitcast_fusion) | copy-start | bytes 16473604
  86.0 17.7 %copy-start.61 = (bf16[25,20,32,512]{3,1,2,0:T(8,128)(2,1)}, bf16[25,20,32,512]{3,1,2,0:T(8,128)(2,1)S(1)}, u32[]{:S(2)}) copy-start(bf16[25,20,32,512]{3,1,2,0:T(8,128)(2,1)S(1)} %get-tuple-element.239) | copy-start | bytes 49152004
  103.6 16.9 %slice-start = ((s8[8110080]{0:T(1024)(128)(4,1)}), s8[4194304]{0:T(1024)(128)(4,1)S(1)}, s32[]{:S(2)}) async-start(s8[8110080]{0:T(1024)(128)(4,1)} %bitcast.2985), calls=%async_computation.2 | async-start | bytes 8388608
  111.4 9.2 slice-start.1
  268.5 10.7 slice-start.4
  269.6 9.6 slice-start.5
  341.6 19.2 %slice-start.6 = ((s8[7077888]{0:T(1024)(128)(4,1)}), s8[4194304]{0:T(1024)(128)(4,1)S(1)}, s32[]{:S(2)}) async-start(s8[7077888]{0:T(1024)(128)(4,1)} %bitcast.2995), calls=%async_computation.8 | async-start | bytes 8388608
  351.3 9.5 slice-start.7
  360.8 76.8 %copy-start.49 = (s32[256]{0:T(256)S(1)}, s32[256]{0:T(256)}, u32[]{:S(2)}) copy-start(s32[256]{0:T(256)} %copy-done.48) | copy-start | bytes 3076
  360.8 76.8 %copy-start.53 = (s32[64]{0:T(128)S(1)}, s32[64]{0:T(128)}, u32[]{:S(2)}) copy-start(s32[64]{0:T(128)} %copy-done.52) | copy-start | bytes 772
  435.3 13.7 %copy-start.40 = (f32[32,512]{1,0:T(8,128)S(1)}, f32[32,512]{1,0:T(8,128)}, u32[]{:S(2)}) copy-start(f32[32,512]{1,0:T(8,128)} %get-tuple-element.555) | copy-start | bytes 196612
  449.0 14.9 %copy-start.9 = (f32[32,512,20]{1,2,0:T(8,128)S(1)}, f32[32,512,20]{1,2,0:T(8,128)}, u32[]{:S(2)}) copy-start(f32[32,512,20]{1,2,0:T(8,128)} %convolution_bitcast_fusion.17) | copy-start | bytes 3932164
  449.1 14.9 %copy-start.35 = (f32[32,512,20]{1,2,0:T(8,128)S(1)}, f32[32,512,20]{1,2,0:T(8,128)}, u32[]{:S(2)}) copy-start(f32[32,512,20]{1,2,0:T(8,128)} %convolution_bitcast_fusion.9) | copy-start | bytes 3932164
  457.8 12.3 %copy-start.8 = (f32[32,512,20]{1,2,0:T(8,128)S(1)}, f32[32,512,20]{1,2,0:T(8,128)}, u32[]{:S(2)}) copy-start(f32[32,512,20]{1,2,0:T(8,128)} %convolution_bitcast_fusion.16) | copy-start | bytes 3932164
  457.9 12.3 %copy-start.33 = (f32[32,512,20]{1,2,0:T(8,128)S(1)}, f32[32,512,20]{1,2,0:T(8,128)}, u32[]{:S(2)}) copy-start(f32[32,512,20]{1,2,0:T(8,128)} %convolution_bitcast_fusion.8) | copy-start | bytes 3932164
  464.0 12.4 %copy-start.7 = (f32[32,512,20]{1,2,0:T(8,128)S(1)}, f32[32,512,20]{1,2,0:T(8,128)}, u32[]{:S(2)}) copy-start(f32[32,512,20]{1,2,0:T(8,128)} %convolution_bitcast_fusion.15) | copy-start | bytes 3932164
  464.0 12.4 %copy-start.28 = (f32[32,512,20]{1,2,0:T(8,128)S(1)}, f32[32,512,20]{1,2,0:T(8,128)}, u32[]{:S(2)}) copy-start(f32[32,512,20]{1,2,0:T(8,128)} %convolution_bitcast_fusion.7) | copy-start | bytes 3932164
  470.2 12.2 %copy-start.11 = (f32[32,512,20]{1,2,0:T(8,128)S(1)}, f32[32,512,20]{1,2,0:T(8,128)}, u32[]{:S(2)}) copy-start(f32[32,512,20]{1,2,0:T(8,128)} %convolution_bitcast_fusion.14) | copy-start | bytes 3932164
  470.2 12.2 %copy-start.26 = (f32[32,512,20]{1,2,0:T(8,128)S(1)}, f32[32,512,20]{1,2,0:T(8,128)}, u32[]{:S(2)}) copy-start(f32[32,512,20]{1,2,0:T(8,128)} %convolution_bitcast_fusion.6) | copy-start | bytes 3932164
  476.4 11.9 %copy-start.25 = (f32[32,512,20]{1,2,0:T(8,128)S(1)}, f32[32,512,20]{1,2,0:T(8,128)}, u32[]{:S(2)}) copy-start(f32[32,512,20]{1,2,0:T(8,128)} %convolution_bitcast_fusion.5) | copy-start | bytes 3932164
  482.4 12.3 %copy-start.24 = (f32[32,512,20]{1,2,0:T(8,128)S(1)}, f32[32,512,20]{1,2,0:T(8,128)}, u32[]{:S(2)}) copy-start(f32[32,512,20]{1,2,0:T(8,128)} %convolution_bitcast_fusion.4) | copy-start | bytes 3932164
  488.4 12.2 %copy-start.10 = (f32[32,512,20]{1,2,0:T(8,128)S(1)}, f32[32,512,20]{1,2,0:T(8,128)}, u32[]{:S(2)}) copy-start(f32[32,512,20]{1,2,0:T(8,128)} %convolution_bitcast_fusion.11) | copy-start | bytes 3932164
  488.4 12.2 %copy-start.29 = (f32[32,512,20]{1,2,0:T(8,128)S(1)}, f32[32,512,20]{1,2,0:T(8,128)}, u32[]{:S(2)}) copy-start(f32[32,512,20]{1,2,0:T(8,128)} %convolution_bitcast_fusion.3) | copy-start | bytes 3932164
  494.7 11.7 %copy-start.45 = (bf16[512,32]{0,1:T(8,128)(2,1)S(1)}, bf16[512,32]{0,1:T(8,128)(2,1)}, u32[]{:S(2)}) copy-start(bf16[512,32]{0,1:T(8,128)(2,1)} %copy-done.44) | copy-start | bytes 98308
  494.7 11.7 %copy-start.47 = (bf16[512,32]{0,1:T(8,128)(2,1)S(1)}, bf16[512,32]{0,1:T(8,128)(2,1)}, u32[]{:S(2)}) copy-start(bf16[512,32]{0,1:T(8,128)(2,1)} %copy-done.46) | copy-start | bytes 98308
  512.3 5.7 collective-permute-start.4
  512.4 5.7 collective-permute-start.5
  522.9 6.1 collective-permute-start.7
  522.9 5.4 collective-permute-start.6
  538.9 11.4 %copy-start.1 = (bf16[20,264,520]{2,1,0:T(8,128)(2,1)}, bf16[20,264,520]{2,1,0:T(8,128)(2,1)S(1)}, u32[]{:S(2)}) copy-start(bf16[20,264,520]{2,1,0:T(8,128)(2,1)S(1)} %maximum_bitcast_fusion.1) | copy-start | bytes 16473604
  563.5 17.7 %slice-start.2 = ((s8[6758400]{0:T(1024)(128)(4,1)}), s8[4194304]{0:T(1024)(128)(4,1)S(1)}, s32[]{:S(2)}) async-start(s8[6758400]{0:T(1024)(128)(4,1)} %bitcast.2987), calls=%async_computation.4 | async-start | bytes 8388608
  571.1 10.1 slice-start.3
  750.7 34.6 %slice-start.14 = ((s8[5898240]{0:T(1024)(128)(4,1)}), s8[4194304]{0:T(1024)(128)(4,1)S(1)}, s32[]{:S(2)}) async-start(s8[5898240]{0:T(1024)(128)(4,1)} %bitcast.3046), calls=%async_computation.16 | async-start | bytes 8388608
  768.0 17.4 %slice-start.15 = ((s8[5898240]{0:T(1024)(128)(4,1)}), s8[1703936]{0:T(1024)(128)(4,1)S(1)}, s32[]{:S(2)}) async-start(s8[5898240]{0:T(1024)(128)(4,1)} %bitcast.3046), calls=%async_computation.17 | async-start | bytes 3407872
  806.8 26.4 %slice-start.18 = ((s8[16384000]{0:T(1024)(128)(4,1)}), s8[4194304]{0:T(1024)(128)(4,1)S(1)}, s32[]{:S(2)}) async-start(s8[16384000]{0:T(1024)(128)(4,1)} %bitcast.3052), calls=%async_computation.20 | async-start | bytes 8388608
  806.8 26.4 %slice-start.19 = ((s8[16384000]{0:T(1024)(128)(4,1)}), s8[4194304]{0:T(1024)(128)(4,1)S(1)}, s32[]{:S(2)}) async-start(s8[16384000]{0:T(1024)(128)(4,1)} %bitcast.3052), calls=%async_computation.21 | async-start | bytes 8388608
  806.8 26.4 %slice-start.20 = ((s8[16384000]{0:T(1024)(128)(4,1)}), s8[4194304]{0:T(1024)(128)(4,1)S(1)}, s32[]{:S(2)}) async-start(s8[16384000]{0:T(1024)(128)(4,1)} %bitcast.3052), calls=%async_computation.22 | async-start | bytes 8388608
  806.8 26.4 %slice-start.21 = ((s8[16384000]{0:T(1024)(128)(4,1)}), s8[3801088]{0:T(1024)(128)(4,1)S(1)}, s32[]{:S(2)}) async-start(s8[16384000]{0:T(1024)(128)(4,1)} %bitcast.3052), calls=%async_computation.23 | async-start | bytes 7602176
  915.6 17.3 %copy-start.62 = (bf16[25,20,32,512]{3,2,1,0:T(8,128)(2,1)S(1)}, bf16[25,20,32,512]{3,2,1,0:T(8,128)(2,1)}, u32[]{:S(2)}) copy-start(bf16[25,20,32,512]{3,2,1,0:T(8,128)(2,1)} %get-tuple-element.501) | copy-start | bytes 49152004
  915.6 27.1 %slice-start.16 = ((s8[5898240]{0:T(1024)(128)(4,1)}), s8[4194304]{0:T(1024)(128)(4,1)S(1)}, s32[]{:S(2)}) async-start(s8[5898240]{0:T(1024)(128)(4,1)} %bitcast.3048), calls=%async_computation.18 | async-start | bytes 8388608
  932.9 9.8 slice-start.17
  947.5 74.3 %copy-start.50 = (s32[256]{0:T(256)S(1)}, s32[256]{0:T(256)}, u32[]{:S(2)}) copy-start(s32[256]{0:T(256)} %copy-done.48) | copy-start | bytes 3076
  947.5 74.3 %copy-start.54 = (s32[64]{0:T(128)S(1)}, s32[64]{0:T(128)}, u32[]{:S(2)}) copy-start(s32[64]{0:T(128)} %copy-done.52) | copy-start | bytes 772
  1026.5 14.7 %copy-start.14 = (f32[32,512,20]{1,2,0:T(8,128)S(1)}, f32[32,512,20]{1,2,0:T(8,128)}, u32[]{:S(2)}) copy-start(f32[32,512,20]{1,2,0:T(8,128)} %fusion.35) | copy-start | bytes 3932164
  1026.5 14.7 %copy-start.32 = (f32[32,512,20]{1,2,0:T(8,128)S(1)}, f32[32,512,20]{1,2,0:T(8,128)}, u32[]{:S(2)}) copy-start(f32[32,512,20]{1,2,0:T(8,128)} %fusion.59) | copy-start | bytes 3932164
  1035.0 12.3 %copy-start.13 = (f32[32,512,20]{1,2,0:T(8,128)S(1)}, f32[32,512,20]{1,2,0:T(8,128)}, u32[]{:S(2)}) copy-start(f32[32,512,20]{1,2,0:T(8,128)} %fusion.38) | copy-start | bytes 3932164
  1035.0 12.3 %copy-start.30 = (f32[32,512,20]{1,2,0:T(8,128)S(1)}, f32[32,512,20]{1,2,0:T(8,128)}, u32[]{:S(2)}) copy-start(f32[32,512,20]{1,2,0:T(8,128)} %fusion.62) | copy-start | bytes 3932164
  1041.2 12.4 %copy-start.12 = (f32[32,512,20]{1,2,0:T(8,128)S(1)}, f32[32,512,20]{1,2,0:T(8,128)}, u32[]{:S(2)}) copy-start(f32[32,512,20]{1,2,0:T(8,128)} %fusion.41) | copy-start | bytes 3932164
  1041.2 12.4 %copy-start.22 = (f32[32,512,20]{1,2,0:T(8,128)S(1)}, f32[32,512,20]{1,2,0:T(8,128)}, u32[]{:S(2)}) copy-start(f32[32,512,20]{1,2,0:T(8,128)} %fusion.65) | copy-start | bytes 3932164
  1047.4 12.4 %copy-start.21 = (f32[32,512,20]{1,2,0:T(8,128)S(1)}, f32[32,512,20]{1,2,0:T(8,128)}, u32[]{:S(2)}) copy-start(f32[32,512,20]{1,2,0:T(8,128)} %fusion.68) | copy-start | bytes 3932164
  1047.4 12.4 %copy-start.31 = (f32[32,512,20]{1,2,0:T(8,128)S(1)}, f32[32,512,20]{1,2,0:T(8,128)}, u32[]{:S(2)}) copy-start(f32[32,512,20]{1,2,0:T(8,128)} %fusion.44) | copy-start | bytes 3932164
  1053.6 12.4 %copy-start.19 = (f32[32,512,20]{1,2,0:T(8,128)S(1)}, f32[32,512,20]{1,2,0:T(8,128)}, u32[]{:S(2)}) copy-start(f32[32,512,20]{1,2,0:T(8,128)} %fusion.71) | copy-start | bytes 3932164
  1053.6 12.4 %copy-start.20 = (f32[32,512,20]{1,2,0:T(8,128)S(1)}, f32[32,512,20]{1,2,0:T(8,128)}, u32[]{:S(2)}) copy-start(f32[32,512,20]{1,2,0:T(8,128)} %fusion.47) | copy-start | bytes 3932164
  1059.8 12.6 %copy-start.17 = (f32[32,512,20]{1,2,0:T(8,128)S(1)}, f32[32,512,20]{1,2,0:T(8,128)}, u32[]{:S(2)}) copy-start(f32[32,512,20]{1,2,0:T(8,128)} %fusion.50) | copy-start | bytes 3932164
  1059.8 12.6 %copy-start.18 = (f32[32,512,20]{1,2,0:T(8,128)S(1)}, f32[32,512,20]{1,2,0:T(8,128)}, u32[]{:S(2)}) copy-start(f32[32,512,20]{1,2,0:T(8,128)} %fusion.74) | copy-start | bytes 3932164
  1066.0 12.3 %copy-start.16 = (f32[32,512,20]{1,2,0:T(8,128)S(1)}, f32[32,512,20]{1,2,0:T(8,128)}, u32[]{:S(2)}) copy-start(f32[32,512,20]{1,2,0:T(8,128)} %fusion.53) | copy-start | bytes 3932164
  1066.0 12.3 %copy-start.23 = (f32[32,512,20]{1,2,0:T(8,128)S(1)}, f32[32,512,20]{1,2,0:T(8,128)}, u32[]{:S(2)}) copy-start(f32[32,512,20]{1,2,0:T(8,128)} %fusion.77) | copy-start | bytes 3932164
  (34 other events, 199.3 us)
Sparse Core Ops, SparseCore 0:
  24.8 129.6 all-reduce.4
  526.5 130.6 all-reduce.6
where the time goes:
time: 1100 us; the launch traced here: 1090 us
  local copies, waits for them, and re-layouts  503 us (46%)
  matrix products  296 us (27%)
  blocking collectives  138 us (13%)
  other arithmetic  123 us (11%)
  between operations  15.5 us (1%)
  starting transfers between devices  13.5 us (1%)
    unnamed x321, local copies, waits for them, and re-layouts  428 us
    dot_general x32, matrix products, conv_rows(): jnp.einsum('otc,tcxy->oxy', shaped_weights, stacked, preferred_element_ty...  255 us
    all_gather x2, blocking collectives, on_device(): gathered = lax.all_gather(own_block, ('gx', 'gy'), axis=0, tiled=True)  138 us
    unnamed x24, other arithmetic  85.4 us
    another operation x9, local copies, waits for them, and re-layouts, conv_rows(): stacked = jnp.stack(pieces, 0)  33.9 us
  transfers between devices with their start and end apart: 10, of which 3 were waited for; matrix products, arithmetic and copies ran while one was open for 70% of the time, Pallas kernels for 0%

commit v1 on v0

v1 whole, which is shorter than its diff:
```python
import math

import jax
import jax.numpy as jnp
from jax import lax
from jax.experimental import pallas as pl
from jax.experimental.pallas import tpu as pltpu
from jax.sharding import PartitionSpec as P

full_turn = 2.0 * math.pi
highest = lax.Precision.HIGHEST
HALO = 4
GROUP = 16
SUB = 8
SLAB = SUB + 2 * HALO


def padded_field(value):
    for axis, dim in (("gx", 1), ("gy", 2)):
        size, length = (lax.axis_size(axis), value.shape[dim])
        up = [(i, (i + 1) % size) for i in range(size)]
        down = [(j, i) for i, j in up]
        last = lax.slice_in_dim(value, length - HALO, length, axis=dim)
        first = lax.slice_in_dim(value, 0, HALO, axis=dim)
        before = lax.ppermute(last, axis, up)
        after = lax.ppermute(first, axis, down)
        pieces = [before, value, after]
        if dim == 1:
            tail = value.shape[:1] + (GROUP - 2 * HALO,) + value.shape[2:]
            pieces.append(jnp.zeros(tail, value.dtype))
        value = jnp.concatenate(pieces, axis=dim)
    return value


def mode_numbers(modes_x, modes_y, cells_x):
    half = modes_x // 2
    lower = jnp.arange(half, dtype=jnp.int32)
    return jnp.concatenate([lower, lower + (cells_x - half)]), jnp.arange(modes_y, dtype=jnp.int32)


def slab_weights(taps, dilation, side):
    channels = taps.shape[0]
    shaped = taps.reshape(channels, side, side, channels)
    out_rows = jnp.arange(SUB)[:, None, None]
    in_rows = jnp.arange(SLAB)[None, :, None]
    offsets = ((jnp.arange(side) - side // 2) * dilation)[None, None, :]
    hit = (in_rows == out_rows + HALO + offsets).astype(taps.dtype)
    full = jnp.einsum("oabc,rsa->orbcs", shaped, hit, preferred_element_type=jnp.float32)
    return full.reshape(channels * SUB, side * channels * SLAB).astype(taps.dtype)


def conv_kernel(u_ref, near_ref, far_ref, mix_ref, bias_ref, out_ref, *, first):
    channels, _, cols = out_ref.shape
    start = pl.multiple_of((pl.program_id(0) + first) * GROUP, GROUP)
    rows = u_ref[:, pl.ds(start, 2 * GROUP), :]
    bias = bias_ref[...]
    for sub in range(GROUP // SUB):
        slab = rows[:, sub * SUB : sub * SUB + SLAB, :].reshape(channels * SLAB, rows.shape[2])
        shifted = {d: slab[:, HALO + d : HALO + d + cols] for d in (-4, -2, -1, 0, 1, 2, 4)}
        near = jnp.dot(
            near_ref[...],
            jnp.concatenate([shifted[d] for d in (-1, 0, 1)], axis=0),
            preferred_element_type=jnp.float32,
        )
        far = jnp.dot(
            far_ref[...],
            jnp.concatenate([shifted[d] for d in (-4, -2, 0, 2, 4)], axis=0),
            preferred_element_type=jnp.float32,
        )
        total = mix_ref[1] * near + mix_ref[2] * far + bias
        out_ref[:, sub * SUB : (sub + 1) * SUB, :] = total.reshape(channels, SUB, cols)


def conv_call(padded, near, far, mixture, bias, rows, cols, first, count):
    channels = padded.shape[0]
    depth = near.shape[1] + far.shape[1]
    vmem = pl.BlockSpec(memory_space=pltpu.VMEM)
    return pl.pallas_call(
        lambda *refs: conv_kernel(*refs, first=first),
        grid=(count,),
        name="conv",
        out_shape=jax.ShapeDtypeStruct((channels, count * GROUP, cols), jnp.float32),
        in_specs=[vmem, vmem, vmem, pl.BlockSpec(memory_space=pltpu.SMEM), vmem],
        out_specs=pl.BlockSpec((channels, GROUP, cols), lambda i: (0, i, 0)),
        cost_estimate=pl.CostEstimate(
            flops=2 * channels * count * GROUP * cols * depth,
            bytes_accessed=channels * count * GROUP * cols * 6,
            transcendentals=0,
        ),
    )(padded, near, far, mixture, bias)


def split_bf16(value):
    high = value.astype(jnp.bfloat16)
    low = (value - high.astype(jnp.float32)).astype(jnp.bfloat16)
    return high, low


def finish_kernel(upper_ref, lower_ref, rows_ref, table_ref, *rest, halves):
    channels, _, cols = upper_ref.shape
    lines = rows_ref[...].reshape(channels * GROUP, rows_ref.shape[2])
    lines_high, lines_low = split_bf16(lines)
    table_high, table_low = split_bf16(table_ref[...])
    spectral = jnp.dot(
        jnp.concatenate([lines_high, lines_low, lines_high], axis=1),
        jnp.concatenate([table_high, table_high, table_low], axis=0),
        preferred_element_type=jnp.float32,
    )
    in_upper = pl.program_id(0) < halves
    conv = jnp.where(in_upper, upper_ref[...], lower_ref[...]).reshape(channels * GROUP, cols)
    value = conv + spectral
    out = (value * 0.5 * (1.0 + lax.erf(value * (0.5**0.5)))).astype(jnp.bfloat16)
    if len(rest) == 3:
        forward_ref, out_ref, lines_ref = rest
        sums = jnp.dot(out, forward_ref[...], preferred_element_type=jnp.float32)
        lines_ref[...] = sums.reshape(lines_ref.shape)
    else:
        (out_ref,) = rest
    out_ref[...] = out.reshape(out_ref.shape)


def finish_call(upper, lower, rows, table, forward):
    channels, upper_rows, cols = upper.shape
    halves = upper_rows // GROUP
    groups = halves + lower.shape[1] // GROUP
    width = rows.shape[2]
    vmem = pl.BlockSpec(memory_space=pltpu.VMEM)
    in_specs = [
        pl.BlockSpec((channels, GROUP, cols), lambda i: (0, jnp.minimum(i, halves - 1), 0)),
        pl.BlockSpec((channels, GROUP, cols), lambda i: (0, jnp.maximum(i - halves, 0), 0)),
        pl.BlockSpec((channels, GROUP, width), lambda i: (0, i, 0)),
        vmem,
    ]
    operands = [upper, lower, rows, table]
    shapes = [jax.ShapeDtypeStruct((channels, groups * GROUP, cols), jnp.bfloat16)]
    out_specs = [pl.BlockSpec((channels, GROUP, cols), lambda i: (0, i, 0))]
    if forward is not None:
        in_specs.append(vmem)
        operands.append(forward)
        shapes.append(jax.ShapeDtypeStruct((channels, groups * GROUP, width), jnp.float32))
        out_specs.append(pl.BlockSpec((channels, GROUP, width), lambda i: (0, i, 0)))
    results = pl.pallas_call(
        lambda *refs: finish_kernel(*refs, halves=halves),
        grid=(groups,),
        name="finish",
        out_shape=shapes,
        in_specs=in_specs,
        out_specs=out_specs,
        cost_estimate=pl.CostEstimate(
            flops=2 * channels * groups * GROUP * cols * 4 * width,
            bytes_accessed=channels * groups * GROUP * cols * 6,
            transcendentals=channels * groups * GROUP * cols,
        ),
    )(*operands)
    return results if forward is not None else (results[0], None)


def solution(mesh):
    def on_device(grid_field, spectral_weight, conv_near, conv_far, mix_logits, channel_bias):
        _, channels, local_rows, local_cols = grid_field.shape
        layers = spectral_weight.shape[0]
        share = spectral_weight.shape[-1]
        devices = lax.axis_size("gx") * lax.axis_size("gy")
        cells_x = local_rows * lax.axis_size("gx")
        cells_y = local_cols * lax.axis_size("gy")
        modes = share * devices
        modes_y = 32
        modes_x = modes // modes_y
        row_modes, col_modes = mode_numbers(modes_x, modes_y, cells_x)
        row_at = lax.axis_index("gx") * local_rows + jnp.arange(local_rows, dtype=jnp.int32)
        col_at = lax.axis_index("gy") * local_cols + jnp.arange(local_cols, dtype=jnp.int32)
        row_phase = (row_at[:, None] * row_modes[None, :] % cells_x).astype(jnp.float32) * (
            full_turn / cells_x
        )
        row_table = jnp.concatenate([jnp.cos(row_phase), jnp.sin(row_phase)], axis=1)
        col_phase = (col_at[:, None] * col_modes[None, :] % cells_y).astype(jnp.float32) * (
            full_turn / cells_y
        )
        col_table = jnp.concatenate([jnp.cos(col_phase), -jnp.sin(col_phase)], axis=1)
        forward = col_table.astype(jnp.bfloat16)
        col_weight = jnp.where(col_modes == 0, 1.0, 2.0).astype(jnp.float32) / (cells_x * cells_y)
        inverse = (col_table * jnp.concatenate([col_weight, col_weight])[None, :]).T
        exponents = jnp.exp(mix_logits)
        mixtures = exponents / jnp.sum(exponents, axis=1, keepdims=True)

        field = grid_field[0]
        lines = jnp.dot(
            field.reshape(channels * local_rows, local_cols),
            forward,
            preferred_element_type=jnp.float32,
        ).reshape(channels, local_rows, 2 * modes_y)
        groups = local_rows // GROUP
        upper_groups = (groups + 1) // 2
        for layer in range(layers):
            near = slab_weights(conv_near[layer], 1, 3)
            far = slab_weights(conv_far[layer], 2, 5)
            bias = jnp.repeat(channel_bias[layer], SUB)[:, None]
            padded = padded_field(field)

            def conv(near, first, count):
                return conv_call(
                    padded, near, far, mixtures[layer], bias, local_rows, local_cols, first, count
                )

            both = jnp.einsum("xj,cxk->jck", row_table, lines, precision=highest)
            cosine, sine = both[:modes_x], both[modes_x:]
            real = cosine[..., :modes_y] + sine[..., modes_y:]
            imaginary = cosine[..., modes_y:] - sine[..., :modes_y]
            partial = jnp.stack([real, imaginary])
            by_owner = partial.transpose(0, 2, 1, 3).reshape(2, channels, devices, share)
            by_owner = by_owner.transpose(2, 0, 1, 3)
            own = lax.psum_scatter(by_owner, ("gx", "gy"), scatter_dimension=0, tiled=True)[0]
            weight = spectral_weight[layer]
            own_real, own_imaginary = own[0][:, None, :], own[1][:, None, :]
            mixed_real = jnp.sum(weight[0] * own_real - weight[1] * own_imaginary, axis=0)
            mixed_imaginary = jnp.sum(weight[0] * own_imaginary + weight[1] * own_real, axis=0)
            own_block = jnp.stack([mixed_real, mixed_imaginary])[None] * mixtures[layer, 0]
            own_block, near_lower = lax.optimization_barrier((own_block, near))
            gathered = lax.all_gather(own_block, ("gx", "gy"), axis=0, tiled=True)
            full = gathered.transpose(1, 2, 0, 3).reshape(2, channels, modes_x, modes_y)
            spread = jnp.concatenate(
                [
                    jnp.concatenate([full[0], full[1]], axis=2),
                    jnp.concatenate([-full[1], full[0]], axis=2),
                ],
                axis=1,
            )
            upper = conv(near, 0, upper_groups)
            lower = conv(near_lower, upper_groups, groups - upper_groups)
            rows = jnp.einsum("xj,cjk->cxk", row_table, spread, precision=highest)
            field, lines = finish_call(
                upper, lower, rows, inverse, forward if layer + 1 < layers else None
            )
        return field[None]

    in_specs = (
        P(None, None, "gx", "gy"),
        P(None, None, None, None, ("gx", "gy")),
        P(),
        P(),
        P(),
        P(),
    )
    return jax.shard_map(
        on_device,
        mesh=mesh,
        in_specs=in_specs,
        out_specs=P(None, None, "gx", "gy"),
        check_vma=False,
    )
```

time: 1100 us -> 545 us (0.50)
  local copies, waits for them, and re-layouts: 503 us -> 84.4 us
  matrix products: 296 us -> 22.6 us
  Pallas kernels: 0 us -> 119 us
  waiting for transfers between devices: 4.62 us -> 105 us
  other arithmetic: 123 us -> 37 us
    unnamed x321 -> x25, local copies, waits for them, and re-layouts: 428 us -> 0.69 us
    dot_general x36 -> x7, matrix products: 279 us -> 20.2 us  [the longest x4 8.42 us: slab_weights(): jnp.einsum('oabc,rsa->orbcs', shaped, hit, preferred_element_type=jnp.flo...]
    pallas_call x0 -> x6, Pallas kernels: none -> 119 us  [the longest x4 87.6 us: conv_call(): pl.pallas_call(lambda *refs: conv_kernel(*refs, first=first), grid=(count...]
    unnamed x4, waiting for transfers between devices: 0.04 us -> 104 us
    unnamed x24 -> x0, other arithmetic: 85.4 us -> none
    convert_element_type x0 -> x9, local copies, waits for them, and re-layouts: none -> 49 us  [the longest x8 48.2 us: slab_weights(): full.reshape(channels * SUB, side * channels * SLAB).astype(taps.dtype)]
    another operation x32 -> x11, local copies, waits for them, and re-layouts: 44.1 us -> 2.03 us  [the longest x2 1.45 us: on_device(): bias = jnp.repeat(channel_bias[layer], SUB)[:, None]]
    concatenate x3 -> x7, other arithmetic: 11.8 us -> 31.3 us  [the longest x4 31 us: padded_field(): value = jnp.concatenate(pieces, axis=dim)]
  transfers between devices with their start and end apart: 10 -> 10, of which waited for: 3 -> 3; matrix products, arithmetic and copies ran while one was open for 70% -> 21% of each run, Pallas kernels for 0% -> 8%
where the time goes in v1:
time: 545 us; the launch traced here: 535 us
  blocking collectives  138 us (25%)
  Pallas kernels  119 us (22%)
  waiting for transfers between devices  105 us (19%)
  local copies, waits for them, and re-layouts  84.4 us (15%)
  other arithmetic  37 us (7%)
  matrix products  22.6 us (4%)
  starting transfers between devices  14.5 us (3%)
  between operations  14.4 us (3%)
    all_gather x2, blocking collectives, on_device(): gathered = lax.all_gather(own_block, ('gx', 'gy'), axis=0, tiled=True)  138 us
    unnamed x4, waiting for transfers between devices  104 us
    pallas_call x4, Pallas kernels, conv_call(): pl.pallas_call(lambda *refs: conv_kernel(*refs, first=first), grid=(count...  87.6 us
    convert_element_type x8, local copies, waits for them, and re-layouts, slab_weights(): full.reshape(channels * SUB, side * channels * SLAB).astype(taps.dtype)  48.2 us
    pallas_call x2, Pallas kernels, finish_call(): pl.pallas_call(lambda *refs: finish_kernel(*refs, halves=halves), grid=(g...  31.1 us
    concatenate x4, other arithmetic, padded_field(): value = jnp.concatenate(pieces, axis=dim)  31 us
    ppermute x4, starting transfers between devices, padded_field(): after = lax.ppermute(first, axis, down)  11.2 us
  transfers between devices with their start and end apart: 10, of which 3 were waited for; matrix products, arithmetic and copies ran while one was open for 21% of the time, Pallas kernels for 8%

profile of v1, /device:TPU:0, one launch (start us, length us, event | category | flops | bytes accessed | tf_op | source)
XLA Modules:
  0.0 534.6 jit_solution(4675572168764827170)
XLA Ops:
  6.8 4.2 fusion.82
  12.0 1.2 fusion.83
  14.2 1.4 copy.61
  15.6 1.7 fusion.77
  17.9 4.0 collective-permute-start.1
  21.9 1.5 fusion.78
  24.9 0.7 multiply_bitcast_fusion.refs_3_
  25.8 2.1 convert_bitcast_fusion.3
  27.9 2.1 convert_bitcast_fusion.2
  30.2 2.7 convert_bitcast_fusion.1
  32.9 1.5 convert_bitcast_fusion
  34.4 0.8 slice_bitcast_fusion
  35.1 4.8 pad_maximum_fusion.3
  40.0 2.3 fusion.75
  42.3 2.6 copy.49
  44.9 2.0 collective-permute-start.2
  46.9 2.6 copy.50
  49.5 1.1 collective-permute-start.3
  51.2 0.8 copy.71.refs_4_
  52.0 5.7 %copy.54 = bf16[20,8,3,20,16]{4,3,2,1,0:T(8,128)(2,1)} copy(bf16[20,8,3,20,16]{3,4,2,0,1:T(8,128)(2,1)} %convert_bitcast_fusion.3) | data formatting | bytes 614400 | tf_op jit(solution)/shard_map/convert_element_type | solution.py:49
  57.7 4.3 convert_element_type.43.refs_1_
  62.0 8.5 %copy.56 = bf16[20,8,5,20,16]{4,3,2,1,0:T(8,128)(2,1)} copy(bf16[20,8,5,20,16]{3,4,2,0,1:T(8,128)(2,1)} %convert_bitcast_fusion.1) | data formatting | bytes 1024000 | tf_op jit(solution)/shard_map/convert_element_type | solution.py:49
  70.4 6.2 %convert_element_type.46.refs_2_ = bf16[160,1600]{1,0:T(8,128)(2,1)} reshape(bf16[20,8,5,20,16]{4,3,2,1,0:T(8,128)(2,1)} %copy.56) | data formatting | bytes 1024000 | tf_op jit(solution)/shard_map/convert_element_type | solution.py:49
  76.7 0.7 broadcast_in_dim_reshape.8.refs_4_
  77.4 5.7 %copy.77 = bf16[20,8,3,20,16]{4,3,2,1,0:T(8,128)(2,1)} copy(bf16[20,8,3,20,16]{3,4,2,0,1:T(8,128)(2,1)} %convert_bitcast_fusion.2) | data formatting | bytes 614400 | tf_op jit(solution)/shard_map/convert_element_type | solution.py:49
  83.1 4.3 convert_element_type.52.refs_1_
  87.4 7.4 %copy.79 = bf16[20,8,5,20,16]{4,3,2,1,0:T(8,128)(2,1)} copy(bf16[20,8,5,20,16]{3,4,2,0,1:T(8,128)(2,1)S(1)} %convert_bitcast_fusion) | data formatting | bytes 1024000 | tf_op jit(solution)/shard_map/convert_element_type | solution.py:49
  94.8 6.2 %convert_element_type.55.refs_2_ = bf16[160,1600]{1,0:T(8,128)(2,1)} reshape(bf16[20,8,5,20,16]{4,3,2,1,0:T(8,128)(2,1)} %copy.79) | data formatting | bytes 1024000 | tf_op jit(solution)/shard_map/convert_element_type | solution.py:49
  101.1 0.7 broadcast_in_dim_reshape.9.refs_4_
  101.8 1.6 copy.51
  103.4 1.6 copy.52
  104.9 10.9 %fusion.1.refs_0_ = bf16[20,272,520]{2,1,0:T(8,128)(2,1)} fusion(bf16[20,8,512]{2,1,0:T(8,128)(2,1)S(1)} %broadcast.109, bf16[20,272,4]{2,1,0:T(8,128)(2,1)S(1)} %copy.52, bf16[20,4,512]{2,1,0:T(4,128)(2,1)} %collective-permute-done.1, bf16[20,256,512]{2,1,0:T(8,128)(2,1)} %bitcast.164, bf16[20,4,512]{2,1,0:T(4,128)(2,1)} %collective-permute-done, ...), kind=kLoop, calls=%fused_computation.5 | loop fusion | flops 33945600 | bytes 11315200 | tf_op jit(solution)/shard_map/concatenate | solution.py:31
  115.8 21.9 %conv.4.refs_0_ = f32[20,128,512]{2,1,0:T(8,128)} custom-call(bf16[20,272,520]{2,1,0:T(8,128)(2,1)} %fusion.1.refs_0_, bf16[160,960]{1,0:T(8,128)(2,1)} %convert_element_type.43.refs_1_, bf16[160,1600]{1,0:T(8,128)(2,1)} %convert_element_type.46.refs_2_, f32[3]{0:T(128)} %get-tuple-element.58.refs_3_, f32[160,1]{1,0:T(8,128)} %broadcast_in_dim_reshape.8.refs_4_), custom_call_target="tpu_custom_call" | custom-call | flops 6710886400 | bytes 7864320 | tf_op jit(solution)/shard_map/conv/pallas_call | solution.py:78
  137.7 10.5 %all-reduce.5.cloned.1.call-done = f32[32,2,20,64]{3,1,2,0:T(2,128)} async-done(((f32[32,2,20,64]{3,1,2,0:T(2,128)}), f32[32,2,20,64]{3,1,2,0:T(2,128)}) %all-reduce.5.cloned.1.call-update) | async-done | bytes 327696
  148.2 0.8 constant_dynamic-slice_fusion.1
  149.8 68.9 %all_gather.6 = f32[32,2,20,64]{3,1,2,0:T(2,128)S(1)} all-gather(f32[1,2,20,64]{3,1,2,0:T(2,128)S(1)} %maximum_multiply_fusion), channel_id=1, replica_groups=mesh['gx'=8,'gy'=4] {'gx','gy'}, dimensions={0}, use_global_device_ids=true | all-gather | bytes 337920 | tf_op jit(solution)/shard_map/all_gather | solution.py:219
  220.1 21.9 %conv.5.refs_1_ = f32[20,128,512]{2,1,0:T(8,128)} custom-call(bf16[20,272,520]{2,1,0:T(8,128)(2,1)} %fusion.1.refs_0_, bf16[160,960]{1,0:T(8,128)(2,1)} %convert_element_type.43.refs_1_, bf16[160,1600]{1,0:T(8,128)(2,1)} %convert_element_type.46.refs_2_, f32[3]{0:T(128)} %get-tuple-element.58.refs_3_, f32[160,1]{1,0:T(8,128)} %broadcast_in_dim_reshape.8.refs_4_), custom_call_target="tpu_custom_call" | custom-call | flops 6710886400 | bytes 7864320 | tf_op jit(solution)/shard_map/conv/pallas_call | solution.py:78
  242.0 3.8 convolution_bitcast_fusion.1.refs_2_
  245.8 16.4 %finish.2 = (bf16[20,256,512]{2,1,0:T(8,128)(2,1)}, f32[20,256,64]{2,1,0:T(8,128)}) custom-call(f32[20,128,512]{2,1,0:T(8,128)} %conv.4.refs_0_, f32[20,128,512]{2,1,0:T(8,128)} %conv.5.refs_1_, f32[20,256,64]{2,1,0:T(8,128)} %convolution_bitcast_fusion.1.refs_2_, f32[64,512]{1,0:T(8,128)} %multiply_bitcast_fusion.refs_3_, bf16[512,64]{1,0:T(8,128)(2,1)} %copy.71.refs_4_), custom_call_target="tpu_custom_call" | custom-call | flops 1342177280 | bytes 15728640 | tf_op jit(solution)/shard_map/finish/pallas_call | solution.py:142
  262.1 2.1 copy.82
  264.3 1.2 fusion.84
  265.5 1.1 fusion.76
  266.6 3.5 collective-permute-start.5
  270.1 0.9 fusion.19
  271.1 1.2 collective-permute-done.4
  272.9 4.8 pad_maximum_fusion.2
  277.7 0.6 fusion.74
  278.3 1.3 copy.72
  279.6 0.7 collective-permute-start.6
  280.3 0.7 copy.73
  281.0 2.5 collective-permute-start.7
  283.5 1.0 maximum_bitcast_fusion.1
  285.2 1.3 copy.84
  286.6 0.7 copy.74
  287.3 1.6 copy.75
  288.9 10.5 %fusion.3.refs_0_ = bf16[20,272,520]{2,1,0:T(8,128)(2,1)} fusion(bf16[20,8,512]{2,1,0:T(8,128)(2,1)S(1)} %broadcast.109, bf16[20,272,4]{2,1,0:T(8,128)(2,1)S(1)} %copy.75, bf16[20,4,512]{2,1,0:T(4,128)(2,1)} %copy-done.7, bf16[20,256,512]{2,1,0:T(8,128)(2,1)} %get-tuple-element.13, bf16[20,4,512]{2,1,0:T(4,128)(2,1)S(1)} %collective-permute-done.4, ...), kind=kLoop, calls=%fused_computation.7 | loop fusion | flops 33945600 | bytes 11315200 | tf_op jit(solution)/shard_map/concatenate | solution.py:31
  299.4 21.9 %conv.6.refs_0_ = f32[20,128,512]{2,1,0:T(8,128)} custom-call(bf16[20,272,520]{2,1,0:T(8,128)(2,1)} %fusion.3.refs_0_, bf16[160,960]{1,0:T(8,128)(2,1)} %convert_element_type.52.refs_1_, bf16[160,1600]{1,0:T(8,128)(2,1)} %convert_element_type.55.refs_2_, f32[3]{0:T(128)} %get-tuple-element.57.refs_3_, f32[160,1]{1,0:T(8,128)} %broadcast_in_dim_reshape.9.refs_4_), custom_call_target="tpu_custom_call" | custom-call | flops 6710886400 | bytes 7864320 | tf_op jit(solution)/shard_map/conv/pallas_call | solution.py:78
  321.4 93.8 %all-reduce.7.cloned.1.call-done = f32[32,2,20,64]{3,1,2,0:T(2,128)} async-done(((f32[32,2,20,64]{3,1,2,0:T(2,128)}), f32[32,2,20,64]{3,1,2,0:T(2,128)}) %all-reduce.7.cloned.1.call-update) | async-done | bytes 327696
  415.2 0.8 constant_dynamic-slice_fusion
  416.2 0.6 maximum_multiply_fusion.1
  416.8 68.7 %all_gather.7 = f32[32,2,20,64]{3,1,2,0:T(2,128)S(1)} all-gather(f32[1,2,20,64]{3,1,2,0:T(2,128)S(1)} %maximum_multiply_fusion.1), channel_id=1, replica_groups=mesh['gx'=8,'gy'=4] {'gx','gy'}, dimensions={0}, use_global_device_ids=true | all-gather | bytes 337920 | tf_op jit(solution)/shard_map/all_gather | solution.py:219
  486.9 21.9 %conv.7.refs_1_ = f32[20,128,512]{2,1,0:T(8,128)} custom-call(bf16[20,272,520]{2,1,0:T(8,128)(2,1)} %fusion.3.refs_0_, bf16[160,960]{1,0:T(8,128)(2,1)} %convert_element_type.52.refs_1_, bf16[160,1600]{1,0:T(8,128)(2,1)} %convert_element_type.55.refs_2_, f32[3]{0:T(128)} %get-tuple-element.57.refs_3_, f32[160,1]{1,0:T(8,128)} %broadcast_in_dim_reshape.9.refs_4_), custom_call_target="tpu_custom_call" | custom-call | flops 6710886400 | bytes 7864320 | tf_op jit(solution)/shard_map/conv/pallas_call | solution.py:78
  508.8 3.8 convolution_bitcast_fusion.refs_2_
  512.6 14.7 %finish.3 = bf16[20,256,512]{2,1,0:T(8,128)(2,1)} custom-call(f32[20,128,512]{2,1,0:T(8,128)} %conv.6.refs_0_, f32[20,128,512]{2,1,0:T(8,128)} %conv.7.refs_1_, f32[20,256,64]{2,1,0:T(8,128)} %convolution_bitcast_fusion.refs_2_, f32[64,512]{1,0:T(8,128)} %multiply_bitcast_fusion.refs_3_), custom_call_target="tpu_custom_call" | custom-call | flops 1342177280 | bytes 15728640 | tf_op jit(solution)/shard_map/finish/pallas_call | solution.py:142
  (97 shorter events, 10.2 us)
Async XLA Ops:
  6.5 141.6 %all-reduce.5.cloned.1.call-start = ((), (), s32[]{:S(2)}) async-start(), calls=%async_computation | async-start | bytes 1310720
  12.0 1.5 copy-start
  12.0 9.9 %copy-start.6 = (f32[2,2,20,20,64]{4,1,3,2,0:T(2,128)S(1)}, f32[2,2,20,20,64]{4,1,3,2,0:T(2,128)}, u32[]{:S(2)}) copy-start(f32[2,2,20,20,64]{4,1,3,2,0:T(2,128)} %param.7) | copy-start | bytes 1228804
  13.2 10.2 %copy-start.10 = (f32[2,3]{1,0:T(2,128)S(1)}, f32[2,3]{1,0:T(2,128)}, u32[]{:S(2)}) copy-start(f32[2,3]{1,0:T(2,128)} %param.10) | copy-start | bytes 76
  13.2 10.4 %copy-start.9 = (bf16[2,20,180]{2,0,1:T(2,128)(2,1)S(1)}, bf16[2,20,180]{2,0,1:T(2,128)(2,1)}, u32[]{:S(2)}) copy-start(bf16[2,20,180]{2,0,1:T(2,128)(2,1)} %param.8) | copy-start | bytes 43204
  13.2 10.7 %copy-start.8 = (bf16[2,20,500]{2,0,1:T(2,128)(2,1)S(1)}, bf16[2,20,500]{2,0,1:T(2,128)(2,1)}, u32[]{:S(2)}) copy-start(bf16[2,20,500]{2,0,1:T(2,128)(2,1)} %param.9) | copy-start | bytes 120004
  15.6 399.6 %all-reduce.7.cloned.1.call-start = ((), (), s32[]{:S(2)}) async-start(), calls=%async_computation.1 | async-start | bytes 1310720
  17.4 17.7 %collective-permute-start = (bf16[20,4,512]{2,1,0:T(4,128)(2,1)}, bf16[20,4,512]{2,1,0:T(4,128)(2,1)}, u32[]{:S(2)}, u32[]{:S(2)}) collective-permute-start(bf16[20,4,512]{2,1,0:T(4,128)(2,1)} %get-tuple-element.31), channel_id=1, source_target_pairs={{0,4},{4,8},{8,12},{12,16},{16,20},{20,24},{24,28},{28,0},{1,5},{5... | collective-permute-start | bytes 245768 | tf_op jit(solution)/shard_map/ppermute | solution.py:25
  17.9 17.3 %collective-permute-start.1 = (bf16[20,4,512]{2,1,0:T(4,128)(2,1)}, bf16[20,4,512]{2,1,0:T(4,128)(2,1)}, u32[]{:S(2)}, u32[]{:S(2)}) collective-permute-start(bf16[20,4,512]{2,1,0:T(4,128)(2,1)} %get-tuple-element.32), channel_id=1, source_target_pairs={{4,0},{8,4},{12,8},{16,12},{20,16},{24,20},{28,24},{0,28},{5,1},{9... | collective-permute-start | bytes 245768 | tf_op jit(solution)/shard_map/ppermute | solution.py:26
  44.9 56.9 %collective-permute-start.2 = (bf16[20,272,4]{1,2,0:T(4,128)(2,1)}, bf16[20,272,4]{1,2,0:T(4,128)(2,1)}, u32[]{:S(2)}, u32[]{:S(2)}) collective-permute-start(bf16[20,272,4]{1,2,0:T(4,128)(2,1)} %copy.49), channel_id=1, source_target_pairs={{0,1},{1,2},{2,3},{3,0},{4,5},{5,6},{6,7},{7,4},{8,9},{9,10},{10,1... | collective-permute-start | bytes 130568 | tf_op jit(solution)/shard_map/ppermute | solution.py:25
  49.5 53.8 %collective-permute-start.3 = (bf16[20,272,4]{1,2,0:T(4,128)(2,1)}, bf16[20,272,4]{1,2,0:T(4,128)(2,1)}, u32[]{:S(2)}, u32[]{:S(2)}) collective-permute-start(bf16[20,272,4]{1,2,0:T(4,128)(2,1)} %copy.50), channel_id=1, source_target_pairs={{1,0},{2,1},{3,2},{0,3},{5,4},{6,5},{7,6},{4,7},{9,8},{10,9},{11,1... | collective-permute-start | bytes 130568 | tf_op jit(solution)/shard_map/ppermute | solution.py:26
  115.8 33.2 %copy-start.4 = (f32[1,1,20,20,64]{4,1,3,2,0:T(1,128)S(1)}, f32[1,1,20,20,64]{4,1,3,2,0:T(1,128)}, u32[]{:S(2)}) copy-start(f32[1,1,20,20,64]{4,1,3,2,0:T(1,128)} %get-tuple-element.34) | copy-start | bytes 307204
  115.8 33.2 %copy-start.5 = (f32[1,1,20,20,64]{4,1,3,2,0:T(1,128)S(1)}, f32[1,1,20,20,64]{4,1,3,2,0:T(1,128)}, u32[]{:S(2)}) copy-start(f32[1,1,20,20,64]{4,1,3,2,0:T(1,128)} %get-tuple-element.35) | copy-start | bytes 307204
  220.1 21.9 %copy-start.1 = (f32[256,128]{1,0:T(8,128)S(1)}, f32[256,128]{1,0:T(8,128)}, u32[]{:S(2)}) copy-start(f32[256,128]{1,0:T(8,128)} %copy-done) | copy-start | bytes 393220
  266.5 5.7 %collective-permute-start.4 = (bf16[20,4,512]{2,1,0:T(4,128)(2,1)S(1)}, bf16[20,4,512]{2,1,0:T(4,128)(2,1)S(1)}, u32[]{:S(2)}, u32[]{:S(2)}) collective-permute-start(bf16[20,4,512]{2,1,0:T(4,128)(2,1)S(1)} %get-tuple-element.29), channel_id=1, source_target_pairs={{0,4},{4,8},{8,12},{12,16},{16,20},{20,24},{24,28},{28,0},{1,5},{5... | collective-permute-start | bytes 245768 | tf_op jit(solution)/shard_map/ppermute | solution.py:25
  266.6 5.7 %collective-permute-start.5 = (bf16[20,4,512]{2,1,0:T(4,128)(2,1)S(1)}, bf16[20,4,512]{2,1,0:T(4,128)(2,1)S(1)}, u32[]{:S(2)}, u32[]{:S(2)}) collective-permute-start(bf16[20,4,512]{2,1,0:T(4,128)(2,1)S(1)} %get-tuple-element.30), channel_id=1, source_target_pairs={{4,0},{8,4},{12,8},{16,12},{20,16},{24,20},{28,24},{0,28},{5,1},{9... | collective-permute-start | bytes 245768 | tf_op jit(solution)/shard_map/ppermute | solution.py:26
  272.3 0.6 copy-start.7
  279.6 7.0 %collective-permute-start.6 = (bf16[20,272,4]{1,2,0:T(4,128)(2,1)}, bf16[20,272,4]{1,2,0:T(4,128)(2,1)S(1)}, u32[]{:S(2)}, u32[]{:S(2)}) collective-permute-start(bf16[20,272,4]{1,2,0:T(4,128)(2,1)} %copy.72), channel_id=1, source_target_pairs={{0,1},{1,2},{2,3},{3,0},{4,5},{5,6},{6,7},{7,4},{8,9},{9,10},{10,1... | collective-permute-start | bytes 130568 | tf_op jit(solution)/shard_map/ppermute | solution.py:25
  281.0 6.3 %collective-permute-start.7 = (bf16[20,272,4]{1,2,0:T(4,128)(2,1)S(1)}, bf16[20,272,4]{1,2,0:T(4,128)(2,1)}, u32[]{:S(2)}, u32[]{:S(2)}) collective-permute-start(bf16[20,272,4]{1,2,0:T(4,128)(2,1)S(1)} %copy.73), channel_id=1, source_target_pairs={{1,0},{2,1},{3,2},{0,3},{5,4},{6,5},{7,6},{4,7},{9,8},{10,9},{11,1... | collective-permute-start | bytes 130568 | tf_op jit(solution)/shard_map/ppermute | solution.py:26
  299.4 116.6 %copy-start.2 = (f32[1,1,20,20,64]{4,1,3,2,0:T(1,128)S(1)}, f32[1,1,20,20,64]{4,1,3,2,0:T(1,128)}, u32[]{:S(2)}) copy-start(f32[1,1,20,20,64]{4,1,3,2,0:T(1,128)} %get-tuple-element.33) | copy-start | bytes 307204
  299.4 116.6 %copy-start.3 = (f32[1,1,20,20,64]{4,1,3,2,0:T(1,128)S(1)}, f32[1,1,20,20,64]{4,1,3,2,0:T(1,128)}, u32[]{:S(2)}) copy-start(f32[1,1,20,20,64]{4,1,3,2,0:T(1,128)} %get-tuple-element.36) | copy-start | bytes 307204
Sparse Core Ops, SparseCore 0:
  15.7 132.4 all-reduce.4
  286.7 128.4 all-reduce.6
